TPU v7x, 32 devices: a whole 2x2x4 slice. The times are simulated.
32 devices in a mesh: layer: 4 (over y, x), ex: 8 (over z, core).
Axes of the slice: x: 2, y: 2, z: 4, core: 2. Of those that a mesh axis runs over, the one named last changes fastest.
Arguments:
- query_factors: bfloat16 [4, 128, 512, 128], P('layer', 'ex'), may hold values from -1.2578125 to 1.2578125
- response_lengths: int32 [128], P('ex'), may hold values from 1 to 512, 32768 in all
- inverse_hessian: float32 [4, 4096, 4096], P('layer', 'ex'), as said below
- stored_gradients: bfloat16 [4, 2048, 4096], P('layer', 'ex'), may hold values from -0.015625 to 0.015625
Outputs:
- scores: float32 [128, 2048], P('layer', 'ex')
Inputs may be any that keep to these rules, and one draw needn't show every extreme that they name: inverse_hessian[l] is symmetric for every layer l.
All inputs are finite; a program needn't handle non-finite values. No bound on the sum of `response_lengths` on one device may be relied on, other than what follows from the above.
Results may differ from a plain program's by a relative error of at most 0.004.
Values may be sent and summed in bfloat16 or wider, within the bound.
A program may use at most 64 MiB of HBM per device.

v0:
```python
import jax
import jax.numpy as jnp
from jax import lax
from jax.sharding import PartitionSpec as P


def form_gradients(query_layer, response_lengths):
    steps = lax.broadcasted_iota(jnp.int32, (query_layer.shape[0], query_layer.shape[1]), 1)
    mask = (steps < response_lengths[:, None]).astype(jnp.bfloat16)
    rank = query_layer.shape[2] // 2
    inputs = query_layer[:, :, :rank] * mask[:, :, None]
    outputs = query_layer[:, :, rank:]
    projected = jnp.einsum("qti,qtj->qij", outputs, inputs, preferred_element_type=jnp.float32)
    return projected.reshape(query_layer.shape[0], rank * rank).astype(jnp.bfloat16)


def per_device(query_factors, response_lengths, inverse_hessian, stored_gradients):
    projected = form_gradients(query_factors[0], response_lengths)
    inverse_rows = inverse_hessian[0]
    stored_layer = stored_gradients[0]
    block_columns = lax.dot_general(
        lax.all_gather(projected, "ex", axis=0, tiled=True).astype(jnp.float32),
        inverse_rows,
        (((1,), (1,)), ((), ())),
        precision=lax.Precision.HIGHEST,
        preferred_element_type=jnp.float32,
    ).astype(jnp.bfloat16)
    layer_total = lax.dot_general(
        lax.all_gather(block_columns, "ex", axis=1, tiled=True),
        stored_layer,
        (((1,), (1,)), ((), ())),
        preferred_element_type=jnp.float32,
    )
    whole = lax.psum(layer_total, "layer")
    share_rows = whole.shape[0] // lax.axis_size("layer")
    return lax.dynamic_slice_in_dim(whole, lax.axis_index("layer") * share_rows, share_rows, 0)


def solution(mesh):
    placed = (P("layer", "ex", None, None), P("ex"), P("layer", "ex", None), P("layer", "ex", None))
    return jax.shard_map(
        per_device, mesh=mesh, in_specs=placed, out_specs=P("layer", "ex"), check_vma=False
    )
```

profile of v0, /device:TPU:0, one launch (start us, length us, event | category | flops | bytes accessed | tf_op | source)
XLA Modules:
  0.0 122.6 jit_solution(9405819389925023810)
XLA Ops:
  6.5 0.0 copy-start
  6.5 0.0 copy-start.1
  6.5 0.0 all-gather.3.cloned.1.call-start
  6.5 4.1 %copy.6 = bf16[1,16,512,128]{2,3,1,0:T(8,128)(2,1)} copy(bf16[1,16,512,128]{3,2,1,0:T(8,128)(2,1)} %param.4) | data formatting | bytes 4194304 | tf_op args[0]
  10.6 0.0 copy-done.1
  10.6 0.1 fusion.10
  10.7 2.0 %fusion.4 = bf16[16,64,64]{1,2,0:T(8,128)(2,1)S(1)} fusion(bf16[16,512,128]{1,2,0:T(8,128)(2,1)} %bitcast.13, bf16[16,512]{1,0:T(8,128)(2,1)S(1)} %fusion.10), kind=kOutput, calls=%fused_computation.5 | convolution fusion | flops 67698688 | bytes 2244608 | tf_op jit(solution)/shard_map/qti,qtj->qij/dot_general | solution.py:13
  12.7 0.2 copy.7
  12.8 0.9 convert_element_type.23
  13.8 0.0 all-gather.3.cloned.1.call-update
  13.8 0.0 all-gather.5.cloned.1.call-start
  13.9 25.1 %all-gather.3.cloned.1.call-done = bf16[128,4096]{1,0:T(8,128)(2,1)} async-done(((bf16[16,4096]{1,0:T(8,128)(2,1)}), bf16[128,4096]{1,0:T(8,128)(2,1)}) %all-gather.3.cloned.1.call-update) | async-done | bytes 1048592 | tf_op jit(solution)/shard_map/all_gather | solution.py:22
  38.9 9.0 %fusion.5 = bf16[128,512]{1,0:T(8,128)(2,1)} fusion(bf16[128,4096]{1,0:T(8,128)(2,1)} %all-gather.3.cloned.1.call-done, f32[1,512,4096]{2,1,0:T(8,128)} %param.6), kind=kOutput, calls=%fused_computation.6 | convolution fusion | flops 3221291008 | bytes 9568256 | tf_op jit(solution)/shard_map/dot_general | solution.py:21
  47.9 0.0 all-gather.5.cloned.1.call-update
  47.9 0.0 all-reduce.2.cloned.1.call-start
  48.0 22.0 %all-gather.5.cloned.1.call-done = bf16[128,4096]{1,0:T(8,128)(2,1)} async-done(((bf16[128,512]{1,0:T(8,128)(2,1)}), bf16[128,4096]{1,0:T(8,128)(2,1)}) %all-gather.5.cloned.1.call-update) | async-done | bytes 1048592 | tf_op jit(solution)/shard_map/all_gather | solution.py:29
  69.9 0.0 copy-done
  69.9 2.7 %fusion.2 = f32[128,256]{1,0:T(8,128)} fusion(bf16[128,4096]{1,0:T(8,128)(2,1)} %all-gather.5.cloned.1.call-done, bf16[1,256,4096]{2,1,0:T(8,128)(2,1)S(1)} %copy-done), kind=kOutput, calls=%fused_computation.2 | convolution fusion | flops 268435456 | bytes 3276800 | tf_op jit(solution)/shard_map/dot_general | solution.py:28
  72.7 0.0 all-reduce.2.cloned.1.call-update
  72.7 42.0 %all-reduce.2.cloned.1.call-done = f32[128,256]{1,0:T(8,128)} async-done(((f32[128,256]{1,0:T(8,128)}), f32[128,256]{1,0:T(8,128)}) %all-reduce.2.cloned.1.call-update) | async-done | bytes 131088 | tf_op jit(solution)/shard_map/psum | solution.py:34
  114.7 1.4 %constant_dynamic-slice_fusion = f32[32,256]{1,0:T(8,128)} fusion(f32[128,256]{1,0:T(8,128)} %all-reduce.2.cloned.1.call-done, s32[]{:T(128)S(6)} %select_n.3), kind=kLoop, calls=%fused_computation.12 | loop fusion | bytes 65540 | tf_op jit(solution)/shard_map/dynamic_slice | solution.py:36
Async XLA Ops:
  6.5 63.4 %copy-start = (bf16[1,256,4096]{2,1,0:T(8,128)(2,1)S(1)}, bf16[1,256,4096]{2,1,0:T(8,128)(2,1)}, u32[]{:S(2)}) copy-start(bf16[1,256,4096]{2,1,0:T(8,128)(2,1)} %param.7) | copy-start | bytes 6291460
  6.5 4.1 %copy-start.1 = (s32[16]{0:T(128)S(1)}, s32[16]{0:T(128)}, u32[]{:S(2)}) copy-start(s32[16]{0:T(128)} %param.5) | copy-start | bytes 196
  6.5 32.4 %all-gather.3.cloned.1.call-start = ((), (), s32[]{:S(2)}) async-start(), calls=%async_computation | async-start | bytes 1179648 | tf_op jit(solution)/shard_map/all_gather | solution.py:22
  13.8 56.1 %all-gather.5.cloned.1.call-start = ((), (), s32[]{:S(2)}) async-start(), calls=%async_computation.1 | async-start | bytes 1179648 | tf_op jit(solution)/shard_map/all_gather | solution.py:29
  47.9 66.8 %all-reduce.2.cloned.1.call-start = ((), (), s32[]{:S(2)}) async-start(), calls=%async_computation.2 | async-start | bytes 262144 | tf_op jit(solution)/shard_map/psum | solution.py:34
Sparse Core Ops, SparseCore 0:
  13.9 24.9 all-gather.2
  48.1 21.8 all-gather.4
  72.8 41.8 all-reduce.1
where the time goes:
time: 123 us
  waiting for transfers between devices  89.1 us (72%)
  matrix products  13.7 us (11%)
  between operations  13.1 us (11%)
  local copies, waits for them, and re-layouts  6.56 us (5%)
    psum x1, waiting for transfers between devices, per_device(): whole = lax.psum(layer_total, 'layer')  42 us
    all_gather x1, waiting for transfers between devices, per_device(): lax.all_gather(projected, 'ex', axis=0, tiled=True).astype(jnp.float32)  25.1 us
    all_gather x1, waiting for transfers between devices, per_device(): lax.all_gather(block_columns, 'ex', axis=1, tiled=True)  22 us
    dot_general x1, matrix products, per_device(): lax.dot_general(lax.all_gather(projected, 'ex', axis=0, tiled=True).astyp...  8.99 us
    unnamed x5, local copies, waits for them, and re-layouts  4.08 us
    dot_general x1, matrix products, per_device(): lax.dot_general(lax.all_gather(block_columns, 'ex', axis=1, tiled=True),...  2.72 us
  transfers between devices with their start and end apart: 3, of which 3 were waited for; matrix products, arithmetic and copies ran while one was open for 0% of the time, Pallas kernels for 0%

commit v1 on v0

v1 whole, which is shorter than its diff:
```python
import functools

import jax
import jax.numpy as jnp
from jax import lax
from jax.experimental import pallas as pl
from jax.experimental.pallas import tpu as pltpu
from jax.sharding import PartitionSpec as P

MESH = pl.DeviceIdType.MESH
NT = (((1,), (1,)), ((), ()))


def form_gradients(query_layer, response_lengths):
    steps = lax.broadcasted_iota(jnp.int32, (query_layer.shape[0], query_layer.shape[1]), 1)
    mask = (steps < response_lengths[:, None]).astype(jnp.bfloat16)
    rank = query_layer.shape[2] // 2
    inputs = query_layer[:, :, :rank] * mask[:, :, None]
    outputs = query_layer[:, :, rank:]
    projected = jnp.einsum("qti,qtj->qij", outputs, inputs, preferred_element_type=jnp.float32)
    return projected.reshape(query_layer.shape[0], rank * rank).astype(jnp.bfloat16)


def per_device_plain(query_factors, response_lengths, inverse_hessian, stored_gradients):
    projected = form_gradients(query_factors[0], response_lengths)
    block_columns = lax.dot_general(
        lax.all_gather(projected, "ex", axis=0, tiled=True).astype(jnp.float32),
        inverse_hessian[0],
        NT,
        precision=lax.Precision.HIGHEST,
        preferred_element_type=jnp.float32,
    ).astype(jnp.bfloat16)
    layer_total = lax.dot_general(
        lax.all_gather(block_columns, "ex", axis=1, tiled=True),
        stored_gradients[0],
        NT,
        preferred_element_type=jnp.float32,
    )
    return lax.psum_scatter(layer_total, "layer", scatter_dimension=0, tiled=True)


class Line:
    def __init__(self, at, chips, chunks, send_sem, recv_sem):
        self.at, self.chips, self.chunks = at, chips, chunks
        self.send_sem, self.recv_sem = send_sem, recv_sem
        e = lax.axis_index("ex")
        self.z, self.c = e // 2, lax.rem(e, 2)

    def source(self, flow, o):
        z = self.z - o if flow == 0 else self.z + o
        return z * 2 + self.c

    def valid(self, flow, o):
        return self.z - o >= 0 if flow == 0 else self.z + o < self.chips

    def copy(self, block, k, send, recv, target):
        ref = self.at(block, k)
        return pltpu.make_async_remote_copy(
            src_ref=ref,
            dst_ref=ref,
            send_sem=self.send_sem.at[send + (k,)],
            recv_sem=self.recv_sem.at[recv + (k,)],
            device_id={"ex": target},
            device_id_type=MESH,
        )

    def onward(self, flow, o, k):
        step = 2 if flow == 0 else -2
        e = self.z * 2 + self.c
        return self.copy(self.source(flow, o), k, (flow, o), (flow, o + 1), e + step)

    def has_next(self, flow):
        return self.z < self.chips - 1 if flow == 0 else self.z > 0

    def aside(self, flow, o, k):
        partner = self.z * 2 + 1 - self.c
        return self.copy(self.source(flow, o), k, (2 + flow, o), (2 + flow, o), partner)

    def arrival(self, flow, o, k, other=False):
        e = self.z * 2 + self.c
        block = self.source(flow, o)
        if other:
            block = block + 1 - 2 * self.c
        row = (2 + flow, o) if other else (flow, o)
        return self.copy(block, k, (0, 0), row, e + 1 - 2 * self.c)

    def start_own(self, k):
        for flow in (0, 1):
            @pl.when(self.has_next(flow))
            def _():
                self.onward(flow, 0, k).start()
        self.aside(0, 0, k).start()

    def relay(self, flow, o, k):
        @pl.when(self.valid(flow, o))
        def _():
            self.arrival(flow, o, k).wait_recv()

            @pl.when(self.has_next(flow))
            def _():
                self.onward(flow, o, k).start()

            self.aside(flow, o, k).start()

    def wait_other(self, flow, o, k):
        self.arrival(flow, o, k, True).wait_recv()

    def finish(self):
        for k in range(self.chunks):
            self.aside(0, 0, k).wait_send()
            for flow in (0, 1):
                for o in range(self.chips):
                    if o:
                        @pl.when(self.valid(flow, o))
                        def _():
                            self.aside(flow, o, k).wait_send()
                    if o < self.chips - 1:
                        @pl.when(jnp.logical_and(self.valid(flow, o), self.has_next(flow)))
                        def _():
                            self.onward(flow, o, k).wait_send()


def kernel(
    chips, layers, ck, cm,
    lens, qf, hess, store, out,
    qv, hv, hhi, hlo, sv, gram, pall, pacc, preall, acc, landed,
    q_sem, h_sem, s_sem, send1, recv1, send2, recv2, send3, recv3,
):
    nq, steps, width = qv.shape
    rank = width // 2
    rows, depth = hv.shape[1], hv.shape[2]
    cores = 2 * chips
    l, e = lax.axis_index("layer"), lax.axis_index("ex")
    z, c = e // 2, lax.rem(e, 2)

    q_copy = pltpu.make_async_copy(qf.at[0], qv, q_sem)
    q_copy.start()
    h_copies = [
        pltpu.make_async_copy(hess.at[0, :, pl.ds(k * depth, depth)], hv.at[k], h_sem.at[k]) for k in range(ck)
    ]
    for copy in h_copies:
        copy.start()
    s_copies = [
        pltpu.make_async_copy(store.at[0, :, pl.ds(d * rows, rows)], sv.at[d], s_sem.at[d]) for d in range(cores)
    ]
    for copy in s_copies:
        copy.start()

    barrier = pltpu.get_barrier_semaphore()
    pl.semaphore_signal(barrier, inc=1, device_id={"ex": e + 1 - 2 * c}, device_id_type=MESH)
    for d in range(1, layers):
        pl.semaphore_signal(barrier, inc=1, device_id={"layer": lax.rem(l + d, layers)}, device_id_type=MESH)

    @pl.when(z > 0)
    def _():
        pl.semaphore_signal(barrier, inc=1, device_id={"ex": e - 2}, device_id_type=MESH)

    @pl.when(z < chips - 1)
    def _():
        pl.semaphore_signal(barrier, inc=1, device_id={"ex": e + 2}, device_id_type=MESH)

    q_copy.wait()
    token = lax.broadcasted_iota(jnp.int32, (steps, width), 0)

    def one_query(q, carry):
        x = qv[q]
        kept = jnp.where(token < lens[q], x.astype(jnp.float32), 0.0).astype(jnp.bfloat16)
        product = lax.dot_general(x, kept, (((0,), (0,)), ((), ())), preferred_element_type=jnp.float32)
        gram[pl.ds(pl.multiple_of(q * rank, rank), rank), :] = product[rank:, :]
        return carry

    lax.fori_loop(0, nq, one_query, 0, unroll=4)
    low = lax.broadcasted_iota(jnp.int32, (nq, width), 1) < rank
    for pair in range(rank // 2):
        even = gram[pl.ds(2 * pair, nq, stride=rank), :]
        odd = gram[pl.ds(2 * pair + 1, nq, stride=rank), :]
        both = jnp.where(low, even, pltpu.roll(odd, rank, 1))
        pall[e, :, pl.ds(pair * width, width)] = both.astype(jnp.bfloat16)

    neighbours = layers + (z > 0).astype(jnp.int32) + (z < chips - 1).astype(jnp.int32)
    pl.semaphore_wait(barrier, neighbours)

    first = Line(lambda b, k: pall.at[b, :, pl.ds(k * depth, depth)], chips, ck, send1, recv1)
    for k in range(ck):
        first.start_own(k)

    strip = 16

    def split(k):
        h_copies[k].wait()

        def body(i, carry):
            at = pl.ds(pl.multiple_of(i * strip, strip), strip)
            whole = hv[k, at, :]
            high = whole.astype(jnp.bfloat16)
            hhi[k, at, :] = high
            hlo[k, at, :] = (whole - high.astype(jnp.float32)).astype(jnp.bfloat16)
            return carry

        lax.fori_loop(0, rows // strip, body, 0)

    for k in range(ck):
        split(k)

    for o in range(1, chips):
        for k in range(ck):
            for flow in (0, 1):
                first.relay(flow, o, k)
            if o == chips - 1:
                first.wait_other(0, 0, k)
                for flow in (0, 1):
                    for p in range(1, chips):
                        @pl.when(first.valid(flow, p))
                        def _():
                            first.wait_other(flow, p, k)
                piece = pall[:, :, k * depth:(k + 1) * depth].reshape(cores * nq, depth)
                term = lax.dot_general(piece, hhi[k], NT, preferred_element_type=jnp.float32)
                term += lax.dot_general(piece, hlo[k], NT, preferred_element_type=jnp.float32)
                if k:
                    term += pacc[...]
                if k < ck - 1:
                    pacc[...] = term
                else:
                    preall[e] = term.astype(jnp.bfloat16)

    part = cores * nq // cm
    second = Line(lambda b, k: preall.at[b, pl.ds(k * part, part), :], chips, cm, send2, recv2)
    for k in range(cm):
        second.start_own(k)

    def scored(block):
        return lax.dot_general(preall[block], sv[block], NT, preferred_element_type=jnp.float32)

    for copy in s_copies:
        copy.wait()
    acc[...] = scored(e)
    for k in range(cm):
        second.wait_other(0, 0, k)
    acc[...] += scored(e + 1 - 2 * c)
    for o in range(1, chips):
        for k in range(cm):
            for flow in (0, 1):
                second.relay(flow, o, k)
        for flow in (0, 1):
            @pl.when(second.valid(flow, o))
            def _():
                acc[...] += scored(second.source(flow, o))
                for k in range(cm):
                    second.wait_other(flow, o, k)
                acc[...] += scored(second.source(flow, o) + 1 - 2 * c)

    share = cores * nq // layers
    copies = []
    for d in range(1, layers):
        target = lax.rem(l + d, layers)
        copy = pltpu.make_async_remote_copy(
            src_ref=acc.at[pl.ds(pl.multiple_of(target * share, share), share), :],
            dst_ref=landed.at[d - 1],
            send_sem=send3.at[d - 1],
            recv_sem=recv3.at[d - 1],
            device_id={"layer": target},
            device_id_type=MESH,
        )
        copy.start()
        copies.append(copy)
    total = acc[pl.ds(pl.multiple_of(l * share, share), share), :]
    for d in range(1, layers):
        copies[d - 1].wait_recv()
        total += landed[d - 1]
    out[...] = total
    for copy in copies:
        copy.wait_send()
    first.finish()
    second.finish()


def per_device(layers, cores, query_factors, response_lengths, inverse_hessian, stored_gradients):
    nq, steps, width = query_factors.shape[1:]
    rows, dim = inverse_hessian.shape[1:]
    examples = stored_gradients.shape[1]
    rank, chips, queries = width // 2, cores // 2, cores * nq
    ck, cm = 4, 4
    depth = dim // ck
    bf16, f32 = jnp.bfloat16, jnp.float32
    hbm = pl.BlockSpec(memory_space=pl.ANY)
    dma = pltpu.SemaphoreType.DMA
    return pl.pallas_call(
        functools.partial(kernel, chips, layers, ck, cm),
        out_shape=jax.ShapeDtypeStruct((queries // layers, examples), f32),
        in_specs=[pl.BlockSpec(memory_space=pltpu.SMEM), hbm, hbm, hbm],
        out_specs=pl.BlockSpec(memory_space=pltpu.VMEM),
        scratch_shapes=[
            pltpu.VMEM((nq, steps, width), bf16),
            pltpu.VMEM((ck, rows, depth), f32),
            pltpu.VMEM((ck, rows, depth), bf16),
            pltpu.VMEM((ck, rows, depth), bf16),
            pltpu.VMEM((cores, examples, rows), bf16),
            pltpu.VMEM((nq * rank, width), f32),
            pltpu.VMEM((cores, nq, dim), bf16),
            pltpu.VMEM((queries, rows), f32),
            pltpu.VMEM((cores, queries, rows), bf16),
            pltpu.VMEM((queries, examples), f32),
            pltpu.VMEM((layers - 1, queries // layers, examples), f32),
            dma,
            dma((ck,)),
            dma((cores,)),
            dma((4, chips, ck)),
            dma((4, chips, ck)),
            dma((4, chips, cm)),
            dma((4, chips, cm)),
            dma((layers - 1,)),
            dma((layers - 1,)),
        ],
        compiler_params=pltpu.CompilerParams(
            collective_id=0, has_side_effects=True, vmem_limit_bytes=56 * 1024 * 1024
        ),
    )(response_lengths, query_factors, inverse_hessian, stored_gradients)


def solution(mesh):
    layers, cores = mesh.shape["layer"], mesh.shape["ex"]
    placed = (P("layer", "ex", None, None), P("ex"), P("layer", "ex", None), P("layer", "ex", None))

    def body(query_factors, response_lengths, inverse_hessian, stored_gradients):
        args = (query_factors, response_lengths, inverse_hessian, stored_gradients)
        if cores % 2 or inverse_hessian.shape[1] % 128 or query_factors.shape[1] % 16:
            return per_device_plain(*args)
        return per_device(layers, cores, *args)

    return jax.shard_map(body, mesh=mesh, in_specs=placed, out_specs=P("layer", "ex"), check_vma=False)
```

time: 123 us -> 46.4 us (0.38)
  waiting for transfers between devices: 89.1 us -> 0 us
  Pallas kernels: 0 us -> 44.9 us
  matrix products: 13.7 us -> 0 us
  between operations: 13.1 us -> 0.01 us
  local copies, waits for them, and re-layouts: 6.56 us -> 1.38 us
    all_gather x2 -> x0, waiting for transfers between devices: 47 us -> none  [the longest x1 25.1 us: per_device(): lax.all_gather(projected, 'ex', axis=0, tiled=True).astype(jnp.float32)]
    pallas_call x0 -> x1, Pallas kernels: none -> 44.9 us  [per_device(): pl.pallas_call(functools.partial(kernel, chips, layers, ck, cm), out_shap...]
    psum x1 -> x0, waiting for transfers between devices: 42 us -> none  [per_device(): whole = lax.psum(layer_total, 'layer')]
    dot_general x3 -> x0, matrix products: 13.7 us -> none  [the longest x1 8.99 us: per_device(): lax.dot_general(lax.all_gather(projected, 'ex', axis=0, tiled=True).astyp...]
    unnamed x5 -> x1, local copies, waits for them, and re-layouts: 4.08 us -> 1.38 us
    dynamic_slice x1 -> x0, local copies, waits for them, and re-layouts: 1.37 us -> none  [per_device(): lax.dynamic_slice_in_dim(whole, lax.axis_index('layer') * share_rows, sha...]
  transfers between devices with their start and end apart: 3 -> 0, of which waited for: 3 -> 0; matrix products, arithmetic and copies ran while one was open for 0% -> 0% of each run, Pallas kernels for 0% -> 0%
where the time goes in v1:
time: 46.4 us; the launch traced here: 46.2 us
  Pallas kernels  44.9 us (97%)
  local copies, waits for them, and re-layouts  1.38 us (3%)
    pallas_call x1, Pallas kernels, per_device(): pl.pallas_call(functools.partial(kernel, chips, layers, ck, cm), out_shap...  44.9 us
    unnamed x1, local copies, waits for them, and re-layouts  1.38 us

profile of v1, /device:TPU:0, one launch (start us, length us, event | category | flops | bytes accessed | tf_op | source)
XLA Modules:
  0.0 46.2 jit_solution(9572947312234844357)
XLA Ops:
  0.0 44.9 %shard_map.46 = f32[32,256]{1,0:T(8,128)} custom-call(s32[16]{0:T(128)} %lens.1, bf16[1,16,512,128]{3,2,1,0:T(8,128)(2,1)} %qf.1, f32[1,512,4096]{2,1,0:T(8,128)} %hess.1, bf16[1,256,4096]{2,1,0:T(8,128)(2,1)} %store.1), custom_call_target="tpu_custom_call" | custom-call | tf_op jit(solution)/shard_map/pallas_call | solution.py:287
  44.9 1.4 %copy.6 = f32[32,256]{1,0:T(8,128)} copy(f32[32,256]{1,0:T(8,128)} %shard_map.46) | data formatting | bytes 65536

commit v2 on v1

--- a/solution.py
+++ b/solution.py
@@ -138,13 +138,9 @@
     h_copies = [
         pltpu.make_async_copy(hess.at[0, :, pl.ds(k * depth, depth)], hv.at[k], h_sem.at[k]) for k in range(ck)
     ]
-    for copy in h_copies:
-        copy.start()
     s_copies = [
         pltpu.make_async_copy(store.at[0, :, pl.ds(d * rows, rows)], sv.at[d], s_sem.at[d]) for d in range(cores)
     ]
-    for copy in s_copies:
-        copy.start()
 
     barrier = pltpu.get_barrier_semaphore()
     pl.semaphore_signal(barrier, inc=1, device_id={"ex": e + 1 - 2 * c}, device_id_type=MESH)
@@ -160,6 +156,8 @@
         pl.semaphore_signal(barrier, inc=1, device_id={"ex": e + 2}, device_id_type=MESH)
 
     q_copy.wait()
+    for copy in h_copies + s_copies:
+        copy.start()
     token = lax.broadcasted_iota(jnp.int32, (steps, width), 0)
 
     def one_query(q, carry):
@@ -202,26 +200,36 @@
     for k in range(ck):
         split(k)
 
+    def product(k):
+        first.wait_other(0, 0, k)
+        for flow in (0, 1):
+            for p in range(1, chips):
+                @pl.when(first.valid(flow, p))
+                def _():
+                    first.wait_other(flow, p, k)
+        piece = pall[:, :, k * depth:(k + 1) * depth].reshape(cores * nq, depth)
+        term = lax.dot_general(piece, hhi[k], NT, preferred_element_type=jnp.float32)
+        term += lax.dot_general(piece, hlo[k], NT, preferred_element_type=jnp.float32)
+        if k:
+            term += pacc[...]
+        if k < ck - 1:
+            pacc[...] = term
+        else:
+            preall[e] = term.astype(jnp.bfloat16)
+
+    farthest = jnp.maximum(z, chips - 1 - z)
     for o in range(1, chips):
         for k in range(ck):
             for flow in (0, 1):
                 first.relay(flow, o, k)
-            if o == chips - 1:
-                first.wait_other(0, 0, k)
-                for flow in (0, 1):
-                    for p in range(1, chips):
-                        @pl.when(first.valid(flow, p))
-                        def _():
-                            first.wait_other(flow, p, k)
-                piece = pall[:, :, k * depth:(k + 1) * depth].reshape(cores * nq, depth)
-                term = lax.dot_general(piece, hhi[k], NT, preferred_element_type=jnp.float32)
-                term += lax.dot_general(piece, hlo[k], NT, preferred_element_type=jnp.float32)
-                if k:
-                    term += pacc[...]
-                if k < ck - 1:
-                    pacc[...] = term
-                else:
-                    preall[e] = term.astype(jnp.bfloat16)
+            if 2 * o >= chips - 1 and k:
+                @pl.when(farthest == o)
+                def _():
+                    product(k - 1)
+        if 2 * o >= chips - 1:
+            @pl.when(farthest == o)
+            def _():
+                product(ck - 1)
 
     part = cores * nq // cm
     second = Line(lambda b, k: preall.at[b, pl.ds(k * part, part), :], chips, cm, send2, recv2)
@@ -233,21 +241,31 @@
 
     for copy in s_copies:
         copy.wait()
-    acc[...] = scored(e)
-    for k in range(cm):
-        second.wait_other(0, 0, k)
-    acc[...] += scored(e + 1 - 2 * c)
+    def own_pair():
+        acc[...] = scored(e)
+        for k in range(cm):
+            second.wait_other(0, 0, k)
+        acc[...] += scored(e + 1 - 2 * c)
+
+    def pair(flow, o):
+        @pl.when(second.valid(flow, o))
+        def _():
+            for k in range(cm):
+                second.wait_other(flow, o, k)
+            acc[...] += scored(second.source(flow, o)) + scored(second.source(flow, o) + 1 - 2 * c)
+
+    work = [own_pair]
     for o in range(1, chips):
         for k in range(cm):
             for flow in (0, 1):
                 second.relay(flow, o, k)
-        for flow in (0, 1):
-            @pl.when(second.valid(flow, o))
-            def _():
-                acc[...] += scored(second.source(flow, o))
-                for k in range(cm):
-                    second.wait_other(flow, o, k)
-                acc[...] += scored(second.source(flow, o) + 1 - 2 * c)
+            if k and work:
+                work.pop(0)()
+        for todo in work:
+            todo()
+        work = [functools.partial(pair, flow, o) for flow in (0, 1)]
+    for todo in work:
+        todo()
 
     share = cores * nq // layers
     copies = []

time: 46.4 us -> 41 us (0.88)
  Pallas kernels: 44.9 us -> 39.4 us
    pallas_call x1, Pallas kernels: 44.9 us -> 39.4 us  [per_device(): pl.pallas_call(functools.partial(kernel, chips, layers, ck, cm), out_shap...]
where the time goes in v2:
time: 41 us; the launch traced here: 40.8 us
  Pallas kernels  39.4 us (96%)
  local copies, waits for them, and re-layouts  1.38 us (3%)
    pallas_call x1, Pallas kernels, per_device(): pl.pallas_call(functools.partial(kernel, chips, layers, ck, cm), out_shap...  39.4 us
    unnamed x1, local copies, waits for them, and re-layouts  1.38 us

profile of v2, /device:TPU:0, one launch (start us, length us, event | category | flops | bytes accessed | tf_op | source)
XLA Modules:
  0.0 40.8 jit_solution(4426691951036004457)
XLA Ops:
  0.0 39.4 %shard_map.46 = f32[32,256]{1,0:T(8,128)} custom-call(s32[16]{0:T(128)} %lens.1, bf16[1,16,512,128]{3,2,1,0:T(8,128)(2,1)} %qf.1, f32[1,512,4096]{2,1,0:T(8,128)} %hess.1, bf16[1,256,4096]{2,1,0:T(8,128)(2,1)} %store.1), custom_call_target="tpu_custom_call" | custom-call | tf_op jit(solution)/shard_map/pallas_call | solution.py:305
  39.4 1.4 %copy.6 = f32[32,256]{1,0:T(8,128)} copy(f32[32,256]{1,0:T(8,128)} %shard_map.46) | data formatting | bytes 65536

commit v3 on v2

--- a/solution.py
+++ b/solution.py
@@ -121,7 +121,7 @@
 
 
 def kernel(
-    chips, layers, ck, cm,
+    chips, layers, ck,
     lens, qf, hess, store, out,
     qv, hv, hhi, hlo, sv, gram, pall, pacc, preall, acc, landed,
     q_sem, h_sem, s_sem, send1, recv1, send2, recv2, send3, recv3,
@@ -231,9 +231,13 @@
             def _():
                 product(ck - 1)
 
-    part = cores * nq // cm
-    second = Line(lambda b, k: preall.at[b, pl.ds(k * part, part), :], chips, cm, send2, recv2)
-    for k in range(cm):
+    share = cores * nq // layers
+
+    def rows_of(k):
+        return pl.ds(pl.multiple_of(lax.rem(l + 1 + k, layers) * share, share), share)
+
+    second = Line(lambda b, k: preall.at[b, rows_of(k), :], chips, layers, send2, recv2)
+    for k in range(layers):
         second.start_own(k)
 
     def scored(block):
@@ -243,48 +247,78 @@
         copy.wait()
     def own_pair():
         acc[...] = scored(e)
-        for k in range(cm):
+        for k in range(layers):
             second.wait_other(0, 0, k)
         acc[...] += scored(e + 1 - 2 * c)
 
     def pair(flow, o):
         @pl.when(second.valid(flow, o))
         def _():
-            for k in range(cm):
+            for k in range(layers):
                 second.wait_other(flow, o, k)
             acc[...] += scored(second.source(flow, o)) + scored(second.source(flow, o) + 1 - 2 * c)
 
+    copies = [
+        pltpu.make_async_remote_copy(
+            src_ref=acc.at[rows_of(k), :],
+            dst_ref=landed.at[k],
+            send_sem=send3.at[k],
+            recv_sem=recv3.at[k],
+            device_id={"layer": lax.rem(l + 1 + k, layers)},
+            device_id_type=MESH,
+        )
+        for k in range(layers - 1)
+    ]
+
+    def last_pairs(o, k):
+        rows = rows_of(k)
+        for flow in (0, 1):
+            @pl.when(second.valid(flow, o))
+            def _():
+                block = second.source(flow, o)
+                acc[rows, :] += lax.dot_general(
+                    preall[block, rows, :], sv[block], NT, preferred_element_type=jnp.float32
+                )
+                second.wait_other(flow, o, k)
+                block = block + 1 - 2 * c
+                acc[rows, :] += lax.dot_general(
+                    preall[block, rows, :], sv[block], NT, preferred_element_type=jnp.float32
+                )
+        if k < layers - 1:
+            copies[k].start()
+
+    def inner_pair(flow, o):
+        @pl.when(farthest != o)
+        def _():
+            pair(flow, o)
+
     work = [own_pair]
     for o in range(1, chips):
-        for k in range(cm):
+        for k in range(layers):
             for flow in (0, 1):
                 second.relay(flow, o, k)
-            if k and work:
+            if work:
                 work.pop(0)()
-        for todo in work:
-            todo()
-        work = [functools.partial(pair, flow, o) for flow in (0, 1)]
-    for todo in work:
-        todo()
-
-    share = cores * nq // layers
-    copies = []
-    for d in range(1, layers):
-        target = lax.rem(l + d, layers)
-        copy = pltpu.make_async_remote_copy(
-            src_ref=acc.at[pl.ds(pl.multiple_of(target * share, share), share), :],
-            dst_ref=landed.at[d - 1],
-            send_sem=send3.at[d - 1],
-            recv_sem=recv3.at[d - 1],
-            device_id={"layer": target},
-            device_id_type=MESH,
-        )
-        copy.start()
-        copies.append(copy)
-    total = acc[pl.ds(pl.multiple_of(l * share, share), share), :]
-    for d in range(1, layers):
-        copies[d - 1].wait_recv()
-        total += landed[d - 1]
+            if k:
+                while work:
+                    work.pop(0)()
+                if 2 * o >= chips - 1:
+                    @pl.when(farthest == o)
+                    def _():
+                        last_pairs(o, k - 1)
+        while work:
+            work.pop(0)()
+        if 2 * o >= chips - 1:
+            @pl.when(farthest == o)
+            def _():
+                last_pairs(o, layers - 1)
+        if o < chips - 1:
+            work = [functools.partial(inner_pair, flow, o) for flow in (0, 1)]
+
+    total = acc[rows_of(layers - 1), :]
+    for k in range(layers - 1):
+        copies[k].wait_recv()
+        total += landed[k]
     out[...] = total
     for copy in copies:
         copy.wait_send()
@@ -297,13 +331,13 @@
     rows, dim = inverse_hessian.shape[1:]
     examples = stored_gradients.shape[1]
     rank, chips, queries = width // 2, cores // 2, cores * nq
-    ck, cm = 4, 4
+    ck = 4
     depth = dim // ck
     bf16, f32 = jnp.bfloat16, jnp.float32
     hbm = pl.BlockSpec(memory_space=pl.ANY)
     dma = pltpu.SemaphoreType.DMA
     return pl.pallas_call(
-        functools.partial(kernel, chips, layers, ck, cm),
+        functools.partial(kernel, chips, layers, ck),
         out_shape=jax.ShapeDtypeStruct((queries // layers, examples), f32),
         in_specs=[pl.BlockSpec(memory_space=pltpu.SMEM), hbm, hbm, hbm],
         out_specs=pl.BlockSpec(memory_space=pltpu.VMEM),
@@ -324,8 +358,8 @@
             dma((cores,)),
             dma((4, chips, ck)),
             dma((4, chips, ck)),
-            dma((4, chips, cm)),
-            dma((4, chips, cm)),
+            dma((4, chips, layers)),
+            dma((4, chips, layers)),
             dma((layers - 1,)),
             dma((layers - 1,)),
         ],
@@ -341,7 +375,8 @@
 
     def body(query_factors, response_lengths, inverse_hessian, stored_gradients):
         args = (query_factors, response_lengths, inverse_hessian, stored_gradients)
-        if cores % 2 or inverse_hessian.shape[1] % 128 or query_factors.shape[1] % 16:
+        shares = query_factors.shape[1] * cores % (16 * layers)
+        if cores % 2 or inverse_hessian.shape[1] % 128 or query_factors.shape[1] % 16 or shares:
             return per_device_plain(*args)
         return per_device(layers, cores, *args)
 

time: 41 us -> 39.9 us (0.973)
  Pallas kernels: 39.4 us -> 38.3 us
    pallas_call x1, Pallas kernels: 39.4 us -> 38.3 us  [per_device(): pl.pallas_call(functools.partial(kernel, chips, layers, ck), out_shape=ja...]
where the time goes in v3:
time: 39.9 us; the launch traced here: 39.7 us
  Pallas kernels  38.3 us (96%)
  local copies, waits for them, and re-layouts  1.38 us (3%)
    pallas_call x1, Pallas kernels, per_device(): pl.pallas_call(functools.partial(kernel, chips, layers, ck), out_shape=ja...  38.3 us
    unnamed x1, local copies, waits for them, and re-layouts  1.38 us

profile of v3, /device:TPU:0, one launch (start us, length us, event | category | flops | bytes accessed | tf_op | source)
XLA Modules:
  0.0 39.7 jit_solution(5278229146322669839)
XLA Ops:
  0.0 38.3 %shard_map.46 = f32[32,256]{1,0:T(8,128)} custom-call(s32[16]{0:T(128)} %lens.1, bf16[1,16,512,128]{3,2,1,0:T(8,128)(2,1)} %qf.1, f32[1,512,4096]{2,1,0:T(8,128)} %hess.1, bf16[1,256,4096]{2,1,0:T(8,128)(2,1)} %store.1), custom_call_target="tpu_custom_call" | custom-call | tf_op jit(solution)/shard_map/pallas_call | solution.py:339
  38.3 1.4 %copy.6 = f32[32,256]{1,0:T(8,128)} copy(f32[32,256]{1,0:T(8,128)} %shard_map.46) | data formatting | bytes 65536

commit v4 on v3

--- a/solution.py
+++ b/solution.py
@@ -197,9 +197,6 @@
 
         lax.fori_loop(0, rows // strip, body, 0)
 
-    for k in range(ck):
-        split(k)
-
     def product(k):
         first.wait_other(0, 0, k)
         for flow in (0, 1):
@@ -222,6 +219,8 @@
         for k in range(ck):
             for flow in (0, 1):
                 first.relay(flow, o, k)
+            if o == 1:
+                split(k)
             if 2 * o >= chips - 1 and k:
                 @pl.when(farthest == o)
                 def _():
@@ -376,7 +375,7 @@
     def body(query_factors, response_lengths, inverse_hessian, stored_gradients):
         args = (query_factors, response_lengths, inverse_hessian, stored_gradients)
         shares = query_factors.shape[1] * cores % (16 * layers)
-        if cores % 2 or inverse_hessian.shape[1] % 128 or query_factors.shape[1] % 16 or shares:
+        if cores < 4 or cores % 2 or inverse_hessian.shape[1] % 128 or query_factors.shape[1] % 16 or shares:
             return per_device_plain(*args)
         return per_device(layers, cores, *args)
 

time: 39.9 us -> 40 us (level)
  no operation moved by 1% of the time
where the time goes in v4:
time: 40 us; the launch traced here: 39.8 us
  Pallas kernels  38.4 us (96%)
  local copies, waits for them, and re-layouts  1.38 us (3%)
    pallas_call x1, Pallas kernels, per_device(): pl.pallas_call(functools.partial(kernel, chips, layers, ck), out_shape=ja...  38.4 us
    unnamed x1, local copies, waits for them, and re-layouts  1.38 us

profile of v4, /device:TPU:0, one launch (start us, length us, event | category | flops | bytes accessed | tf_op | source)
XLA Modules:
  0.0 39.8 jit_solution(10492401800999976349)
XLA Ops:
  0.0 38.4 %shard_map.46 = f32[32,256]{1,0:T(8,128)} custom-call(s32[16]{0:T(128)} %lens.1, bf16[1,16,512,128]{3,2,1,0:T(8,128)(2,1)} %qf.1, f32[1,512,4096]{2,1,0:T(8,128)} %hess.1, bf16[1,256,4096]{2,1,0:T(8,128)(2,1)} %store.1), custom_call_target="tpu_custom_call" | custom-call | tf_op jit(solution)/shard_map/pallas_call | solution.py:338
  38.4 1.4 %copy.6 = f32[32,256]{1,0:T(8,128)} copy(f32[32,256]{1,0:T(8,128)} %shard_map.46) | data formatting | bytes 65536
